TPU v7x, 512 devices: a whole 4x4x16 slice. The times are simulated.
512 devices in a mesh: row: 32 (over z, core), col: 16 (over x, y).
Axes of the slice: x: 4, y: 4, z: 16, core: 2. Of those that a mesh axis runs over, the one named last changes fastest.
Arguments:
- trailing: float32 [16384, 16384], P('row', 'col'), may hold values from -6 to 6
- panel: float32 [16384, 512], P(('row', 'col')), may hold values from -0.25 to 0.25
- inv_factor: float32 [512, 512], P(None, 'col'), as said below
- later_series: float32 [16384, 1024], P('row', 'col'), may hold values from -6 to 6
- fold_series: float32 [512, 1024], P('row', 'col'), may hold values from -6 to 6
- fold_len: int32 [1024], P('col'), may hold values from 1 to 32, as said below
Outputs:
- new_trailing: float32 [16384, 16384], P('row', 'col')
- new_series: float32 [16384, 1024], P('row', 'col')
Inputs may be any that keep to these rules, and one draw needn't show every extreme that they name: inv_factor is lower triangular with a diagonal between 1 and 2. `fold_len`: some series reach all 32 blocks and some only one.
All inputs are finite; a program needn't handle non-finite values.
Results may differ from a plain program's by a relative error of at most 0.0003.
Values sent between devices are 32-bit elements; how exact they have to be, the bound alone decides.
No kernel may reach another device: no remote copies, remote signals or barrier semaphores. Data moves between devices by JAX's collectives and lax.ppermute only.
A program may use at most 64 MiB of HBM per device.

v0:
```python
import jax
import jax.numpy as jnp
from jax import lax
from jax.sharding import PartitionSpec as P


def spread(array, axis, root):
    mine = lax.axis_index(axis) == root
    return lax.psum(jnp.where(mine, array, jnp.zeros_like(array)), axis)


def on_device(trailing, panel, inv_factor, later_series, fold_series, fold_len):
    highest = lax.Precision.HIGHEST
    contract = (((1,), (1,)), ((), ()))
    inverse = lax.all_gather(inv_factor, "col", axis=1, tiled=True)
    solved_mine = lax.dot_general(
        panel, inverse, contract, precision=highest, preferred_element_type=jnp.float32
    )
    row_block = lax.all_gather(solved_mine, "col", axis=0, tiled=True)
    rows_here = trailing.shape[0]
    cols_here = trailing.shape[1]
    tiles_across = cols_here // rows_here
    row_pos = lax.axis_index("row")
    col_pos = lax.axis_index("col")
    pieces = []
    for offset in range(tiles_across):
        source = col_pos * tiles_across + offset
        pieces.append(spread(row_block, "row", source))
    col_panel = jnp.concatenate(pieces, 0)
    update = lax.dot_general(
        row_block, col_panel, contract, precision=highest, preferred_element_type=jnp.float32
    )
    col_tile = (col_pos * cols_here + jnp.arange(cols_here, dtype=jnp.int32)) // rows_here
    lower = col_tile <= row_pos
    new_trailing = jnp.where(lower[None, :], trailing - update, trailing)
    fold_all = lax.all_gather(fold_series, "row", axis=0, tiled=True)
    innovations = jnp.dot(inverse, fold_all, precision=highest, preferred_element_type=jnp.float32)
    correction = jnp.dot(
        row_block, innovations, precision=highest, preferred_element_type=jnp.float32
    )
    active = row_pos < fold_len
    new_series = jnp.where(active[None, :], later_series - correction, later_series)
    return (new_trailing, new_series)


def solution(mesh):
    in_specs = (
        P("row", "col"),
        P(("row", "col"), None),
        P(None, "col"),
        P("row", "col"),
        P("row", "col"),
        P("col"),
    )
    out_specs = (P("row", "col"), P("row", "col"))
    return jax.shard_map(
        on_device, mesh=mesh, in_specs=in_specs, out_specs=out_specs, check_vma=False
    )
```

profile of v0, /device:TPU:1, one launch (start us, length us, event | category | flops | bytes accessed | tf_op | source)
XLA Modules:
  0.0 367.0 jit_solution(11055402713785752273)
XLA Ops:
  7.2 0.0 copy-start
  7.2 0.0 all-gather.3.cloned.1.call-start
  7.2 0.7 all-gather.3.cloned.1.call-update
  7.9 0.0 all-gather.5.cloned.1.call-start
  8.0 64.4 %all-gather.3.cloned.1.call-done = f32[512,512]{0,1:T(8,128)} async-done(((f32[512,32]{0,1:T(8,128)}), f32[512,512]{0,1:T(8,128)}) %all-gather.3.cloned.1.call-update) | async-done | bytes 1048592 | tf_op jit(solution)/shard_map/all_gather | solution.py:15
  72.3 0.0 copy-done
  72.3 2.6 fusion.12
  74.9 0.0 all-gather.5.cloned.1.call-update
  74.9 0.0 all-reduce.3.cloned.1.call-start
  75.0 0.0 copy-start.4
  75.0 0.0 copy-start.5
  75.0 0.0 copy-start.2
  75.0 58.2 %all-gather.5.cloned.1.call-done = f32[512,512]{1,0:T(8,128)} async-done(((f32[32,512]{1,0:T(8,128)}), f32[512,512]{1,0:T(8,128)}) %all-gather.5.cloned.1.call-update) | async-done | bytes 1048592 | tf_op jit(solution)/shard_map/all_gather | solution.py:19
  133.2 2.8 broadcast_select_fusion.1
  136.0 0.0 copy-start.1
  136.0 0.0 copy-start.3
  136.0 0.0 all-reduce.3.cloned.1.call-update
  136.1 0.0 copy-done.4
  136.1 34.2 %all_gather.11 = f32[512,64]{1,0:T(8,128)S(1)} all-gather(f32[16,64]{1,0:T(8,128)S(1)} %copy-done.4), channel_id=1, replica_groups=mesh['row'=32,'col'=16] {'row'}, dimensions={0}, use_global_device_ids=true | all-gather | bytes 135168 | tf_op jit(solution)/shard_map/all_gather | solution.py:36
  170.3 0.0 copy-done.5
  170.3 0.0 copy-done.2
  170.3 1.8 fusion.13
  172.1 0.0 copy-done.1
  172.1 0.0 copy-done.3
  172.1 1.8 fusion.6
  174.0 179.8 %all-reduce.3.cloned.1.call-done = (f32[512,512]{1,0:T(8,128)}, f32[512,512]{1,0:T(8,128)}) async-done(((f32[512,512]{1,0:T(8,128)}, f32[512,512]{1,0:T(8,128)}), (f32[512,512]{1,0:T(8,128)}, f32[512,512]{1,0:T(8,128)})) %all-reduce.3.cloned.1.call-update) | async-done | bytes 2097168 | tf_op jit(solution)/shard_map/psum | solution.py:9
  353.7 6.7 %subtract_select_fusion = f32[512,1024]{1,0:T(8,128)} fusion(f32[512,1024]{1,0:T(8,128)} %param.6, f32[512,512]{1,0:T(8,128)S(1)} %copy-done.1, f32[512,512]{1,0:T(8,128)} %get-tuple-element.2, f32[512,512]{1,0:T(8,128)} %get-tuple-element.3, pred[1024]{0:T(1024)(128)(4,1)S(1)} %fusion.8), kind=kOutput, calls=%fused_computation | convolution fusion | flops 3222798336 | bytes 7341056 | tf_op jit(solution)/shard_map/dot_general | solution.py:30
  (2 shorter events, 0.0 us)
Async XLA Ops:
  7.2 65.2 %copy-start = (f32[32,512]{1,0:T(8,128)S(1)}, f32[32,512]{1,0:T(8,128)}, u32[]{:S(2)}) copy-start(f32[32,512]{1,0:T(8,128)} %param.7) | copy-start | bytes 196612
  7.2 65.1 %all-gather.3.cloned.1.call-start = ((), (), s32[]{:S(2)}) async-start(), calls=%async_computation | async-start | bytes 1114112 | tf_op jit(solution)/shard_map/all_gather | solution.py:15
  7.9 125.3 %all-gather.5.cloned.1.call-start = ((), (), s32[]{:S(2)}) async-start(), calls=%async_computation.1 | async-start | bytes 1114112 | tf_op jit(solution)/shard_map/all_gather | solution.py:19
  74.9 278.8 %all-reduce.3.cloned.1.call-start = ((), (), s32[]{:S(2)}) async-start(), calls=%async_computation.2 | async-start | bytes 4194304 | tf_op jit(solution)/shard_map/psum | solution.py:9
  75.0 61.1 %copy-start.4 = (f32[16,64]{1,0:T(8,128)S(1)}, f32[16,64]{1,0:T(8,128)}, u32[]{:S(2)}) copy-start(f32[16,64]{1,0:T(8,128)} %param.10) | copy-start | bytes 12292
  75.0 95.3 %copy-start.5 = (s32[64]{0:T(128)S(1)}, s32[64]{0:T(128)}, u32[]{:S(2)}) copy-start(s32[64]{0:T(128)} %param.11) | copy-start | bytes 772
  75.0 95.3 %copy-start.2 = (f32[512,512]{0,1:T(8,128)S(1)}, f32[512,512]{0,1:T(8,128)}, u32[]{:S(2)}) copy-start(f32[512,512]{0,1:T(8,128)} %all-gather.3.cloned.1.call-done) | copy-start | bytes 3145732
  136.0 36.1 %copy-start.1 = (f32[512,512]{1,0:T(8,128)S(1)}, f32[512,512]{1,0:T(8,128)}, u32[]{:S(2)}) copy-start(f32[512,512]{1,0:T(8,128)} %all-gather.5.cloned.1.call-done) | copy-start | bytes 3145732
  136.0 36.1 %copy-start.3 = (f32[512,64]{0,1:T(8,128)S(1)}, f32[512,64]{0,1:T(8,128)}, u32[]{:S(2)}) copy-start(f32[512,64]{0,1:T(8,128)} %param.9) | copy-start | bytes 393220
Sparse Core Ops, SparseCore 0:
  11.0 61.2 all-gather.2
  75.9 57.2 all-gather.4
  136.2 217.5 all-reduce.2
where the time goes:
time: 367 us
  waiting for transfers between devices  303 us (83%)
  blocking collectives  34.2 us (9%)
  between operations  13.8 us (4%)
  matrix products  12.9 us (4%)
    psum x1, waiting for transfers between devices, spread(): return lax.psum(jnp.where(mine, array, jnp.zeros_like(array)), axis)  180 us
    all_gather x1, waiting for transfers between devices, on_device(): inverse = lax.all_gather(inv_factor, 'col', axis=1, tiled=True)  64.4 us
    all_gather x1, waiting for transfers between devices, on_device(): row_block = lax.all_gather(solved_mine, 'col', axis=0, tiled=True)  58.2 us
    all_gather x1, blocking collectives, on_device(): fold_all = lax.all_gather(fold_series, 'row', axis=0, tiled=True)  34.2 us
  transfers between devices with their start and end apart: 3, of which 3 were waited for; matrix products, arithmetic and copies ran while one was open for 1% of the time, Pallas kernels for 0%

commit v1 on v0

--- a/solution.py
+++ b/solution.py
@@ -2,6 +2,12 @@
 import jax.numpy as jnp
 from jax import lax
 from jax.sharding import PartitionSpec as P
+
+
+def gather_from_all(x, axis, dim):
+    count = lax.axis_size(axis)
+    repeats = [count if d == dim else 1 for d in range(x.ndim)]
+    return lax.all_to_all(jnp.tile(x, repeats), axis, split_axis=dim, concat_axis=dim, tiled=True)
 
 
 def spread(array, axis, root):
@@ -16,7 +22,7 @@
     solved_mine = lax.dot_general(
         panel, inverse, contract, precision=highest, preferred_element_type=jnp.float32
     )
-    row_block = lax.all_gather(solved_mine, "col", axis=0, tiled=True)
+    row_block = gather_from_all(solved_mine, "col", 0)
     rows_here = trailing.shape[0]
     cols_here = trailing.shape[1]
     tiles_across = cols_here // rows_here

time: 367 us -> 327 us (0.89)
  waiting for transfers between devices: 303 us -> 258 us
  starting transfers between devices: 0.12 us -> 4.45 us
    all_gather x1 -> x0, waiting for transfers between devices: 58.2 us -> none  [on_device(): row_block = lax.all_gather(solved_mine, 'col', axis=0, tiled=True)]
    all_to_all x0 -> x1, waiting for transfers between devices: none -> 14.2 us  [gather_from_all(): lax.all_to_all(jnp.tile(x, repeats), axis, split_axis=dim, concat_axis=di...]
    all_to_all x0 -> x1, starting transfers between devices: none -> 4.37 us  [gather_from_all(): lax.all_to_all(jnp.tile(x, repeats), axis, split_axis=dim, concat_axis=di...]
where the time goes in v1:
time: 327 us
  waiting for transfers between devices  258 us (79%)
  blocking collectives  35.5 us (11%)
  between operations  14.1 us (4%)
  matrix products  12.2 us (4%)
  starting transfers between devices  4.45 us (1%)
    psum x1, waiting for transfers between devices, spread(): return lax.psum(jnp.where(mine, array, jnp.zeros_like(array)), axis)  179 us
    all_gather x1, waiting for transfers between devices, on_device(): inverse = lax.all_gather(inv_factor, 'col', axis=1, tiled=True)  64.4 us
    all_gather x1, blocking collectives, on_device(): fold_all = lax.all_gather(fold_series, 'row', axis=0, tiled=True)  35.5 us
    all_to_all x1, waiting for transfers between devices, gather_from_all(): lax.all_to_all(jnp.tile(x, repeats), axis, split_axis=dim, concat_axis=di...  14.2 us
    dot_general x1, matrix products, on_device(): lax.dot_general(row_block, col_panel, contract, precision=highest, prefer...  6.69 us
  transfers between devices with their start and end apart: 3, of which 3 were waited for; matrix products, arithmetic and copies ran while one was open for 1% of the time, Pallas kernels for 0%

profile of v1, /device:TPU:1, one launch (start us, length us, event | category | flops | bytes accessed | tf_op | source)
XLA Modules:
  0.0 327.0 jit_solution(6694178178313173914)
XLA Ops:
  7.2 0.0 copy-start
  7.2 0.0 all-gather.2.cloned.1.call-start
  7.2 0.7 all-gather.2.cloned.1.call-update
  7.9 64.4 %all-gather.2.cloned.1.call-done = f32[512,512]{0,1:T(8,128)} async-done(((f32[512,32]{0,1:T(8,128)}), f32[512,512]{0,1:T(8,128)}) %all-gather.2.cloned.1.call-update) | async-done | bytes 1048592 | tf_op jit(solution)/shard_map/all_gather | solution.py:21
  72.3 0.0 copy-done
  72.3 1.9 fusion.12
  74.3 1.1 tile.2
  75.4 4.4 %all-to-all-start = ((f32[16,32,512]{2,1,0:T(8,128)}), f32[16,32,512]{2,1,0:T(8,128)S(1)}, u32[]{:S(2)}, u32[]{:S(2)}) async-start(f32[16,32,512]{2,1,0:T(8,128)} %tile.2), calls=%async_computation | async-start | bytes 2097152 | tf_op jit(solution)/shard_map/all_to_all | solution.py:10
  79.7 0.0 all-reduce.3.cloned.1.call-start
  79.8 0.0 copy-start.3
  79.8 0.0 copy-start.4
  79.8 0.0 copy-start.1
  79.8 14.2 %all-to-all-done = f32[16,32,512]{2,1,0:T(8,128)S(1)} async-done(((f32[16,32,512]{2,1,0:T(8,128)}), f32[16,32,512]{2,1,0:T(8,128)S(1)}, u32[]{:S(2)}, u32[]{:S(2)}) %all-to-all-start) | async-done | bytes 1048608 | tf_op jit(solution)/shard_map/all_to_all | solution.py:10
  94.0 1.6 broadcast_select_fusion.1
  95.6 0.0 copy-start.2
  95.6 0.0 all-reduce.3.cloned.1.call-update
  95.6 0.0 copy-done.3
  95.6 35.5 %all_gather.7 = f32[512,64]{1,0:T(8,128)S(1)} all-gather(f32[16,64]{1,0:T(8,128)S(1)} %copy-done.3), channel_id=1, replica_groups=mesh['row'=32,'col'=16] {'row'}, dimensions={0}, use_global_device_ids=true | all-gather | bytes 135168 | tf_op jit(solution)/shard_map/all_gather | solution.py:42
  131.2 0.0 copy-done.4
  131.2 0.0 copy-done.1
  131.2 1.8 fusion.13
  133.0 0.0 copy-done.2
  133.0 1.8 fusion.6
  134.8 178.6 %all-reduce.3.cloned.1.call-done = (f32[512,512]{1,0:T(8,128)}, f32[512,512]{1,0:T(8,128)}) async-done(((f32[512,512]{1,0:T(8,128)}, f32[512,512]{1,0:T(8,128)}), (f32[512,512]{1,0:T(8,128)}, f32[512,512]{1,0:T(8,128)})) %all-reduce.3.cloned.1.call-update) | async-done | bytes 2097168 | tf_op jit(solution)/shard_map/psum | solution.py:15
  313.4 6.7 %subtract_select_fusion = f32[512,1024]{1,0:T(8,128)} fusion(f32[512,1024]{1,0:T(8,128)} %param.6, f32[512,512]{1,0:T(8,128)S(1)} %bitcast.11, f32[512,512]{1,0:T(8,128)} %get-tuple-element.2, f32[512,512]{1,0:T(8,128)} %get-tuple-element.3, pred[1024]{0:T(1024)(128)(4,1)S(1)} %fusion.8), kind=kOutput, calls=%fused_computation | convolution fusion | flops 3222798336 | bytes 7341056 | tf_op jit(solution)/shard_map/dot_general | solution.py:36
  (2 shorter events, 0.0 us)
Async XLA Ops:
  7.2 65.2 %copy-start = (f32[32,512]{1,0:T(8,128)S(1)}, f32[32,512]{1,0:T(8,128)}, u32[]{:S(2)}) copy-start(f32[32,512]{1,0:T(8,128)} %param.7) | copy-start | bytes 196612
  7.2 65.1 %all-gather.2.cloned.1.call-start = ((), (), s32[]{:S(2)}) async-start(), calls=%async_computation.1 | async-start | bytes 1114112 | tf_op jit(solution)/shard_map/all_gather | solution.py:21
  75.4 18.7 %all-to-all-start = ((f32[16,32,512]{2,1,0:T(8,128)}), f32[16,32,512]{2,1,0:T(8,128)S(1)}, u32[]{:S(2)}, u32[]{:S(2)}) async-start(f32[16,32,512]{2,1,0:T(8,128)} %tile.2), calls=%async_computation | async-start | bytes 2097152 | tf_op jit(solution)/shard_map/all_to_all | solution.py:10
  79.7 233.7 %all-reduce.3.cloned.1.call-start = ((), (), s32[]{:S(2)}) async-start(), calls=%async_computation.2 | async-start | bytes 4194304 | tf_op jit(solution)/shard_map/psum | solution.py:15
  79.8 15.8 %copy-start.3 = (f32[16,64]{1,0:T(8,128)S(1)}, f32[16,64]{1,0:T(8,128)}, u32[]{:S(2)}) copy-start(f32[16,64]{1,0:T(8,128)} %param.10) | copy-start | bytes 12292
  79.8 51.3 %copy-start.4 = (s32[64]{0:T(128)S(1)}, s32[64]{0:T(128)}, u32[]{:S(2)}) copy-start(s32[64]{0:T(128)} %param.11) | copy-start | bytes 772
  79.8 51.4 %copy-start.1 = (f32[512,512]{0,1:T(8,128)S(1)}, f32[512,512]{0,1:T(8,128)}, u32[]{:S(2)}) copy-start(f32[512,512]{0,1:T(8,128)} %all-gather.2.cloned.1.call-done) | copy-start | bytes 3145732
  95.6 37.4 %copy-start.2 = (f32[512,64]{0,1:T(8,128)S(1)}, f32[512,64]{0,1:T(8,128)}, u32[]{:S(2)}) copy-start(f32[512,64]{0,1:T(8,128)} %param.9) | copy-start | bytes 393220
Sparse Core Ops, SparseCore 0:
  11.0 61.2 all-gather.1
  95.7 217.6 all-reduce.2
